TPU v7x, 256 devices: a whole 4x4x8 slice. The times are simulated.
256 devices in a mesh: dp: 8 (over y, z_lo), owner: 32 (over x, z_hi, core).
Axes of the slice: x: 4, y: 4, z: 8 (z_hi: 4, z_lo: 2; z = z_hi * 2 + z_lo), core: 2. Of those that a mesh axis runs over, the one named last changes fastest.
Arguments:
- partials: bfloat16 [256, 96, 128, 128], P(('dp', 'owner')), may hold values from -1.75 to 1.75
- owners: int32 [96], replicated, may hold values from 0 to 31, as said below
- step_count: int32 [1], replicated, may hold values from 1 to 49
- master: float32 [192, 128, 128], P('owner'), may hold values from -0.3125 to 0.3125
- moment: float32 [192, 128, 128], P('owner'), may hold values from -4 to 4
- second: float32 [192, 128, 128], P('owner'), may hold values from 0.1 to 10
- stat_left: float32 [192, 128, 128], P('owner'), may hold values from -1.5 to 82
- stat_right: float32 [192, 128, 128], P('owner'), may hold values from -1.5 to 82
- basis_left: float32 [192, 128, 128], P('owner'), may hold values from -0.12 to 1.12
- basis_right: float32 [192, 128, 128], P('owner'), may hold values from -0.12 to 1.12
Outputs:
- weights_all: bfloat16 [96, 128, 128], replicated
- direction: float32 [192, 128, 128], P('owner')
- left_new: float32 [192, 128, 128], P('owner')
- right_new: float32 [192, 128, 128], P('owner')
Inputs may be any that keep to these rules, and one draw needn't show every extreme that they name: `owners`: each owner index is named by at least one and at most 6 blocks, and some index by exactly 6.
All inputs are finite; a program needn't handle non-finite values.
Results may differ from a plain program's by a relative error of at most 0.0065.
Values may be sent and summed in bfloat16 or wider, within the bound.
A program may use at most 128 MiB of HBM per device.

v0:
```python
import jax
import jax.numpy as jnp
from jax import lax
from jax.sharding import PartitionSpec as P

NS_ITERS = 6


def product(left, right):
    return jnp.matmul(left, right, precision=lax.Precision.HIGHEST)


def transposed(array):
    return jnp.swapaxes(array, 1, 2)


def refresh(stat, basis):
    power = product(stat, basis)
    magnitude = jnp.sqrt(jnp.sum(power * power, axis=(1, 2), keepdims=True))
    iterate = power / (magnitude + 1e-06)
    for repeat_count in range(NS_ITERS):
        iterate = 1.5 * iterate - 0.5 * product(iterate, product(transposed(iterate), iterate))
    return iterate


def slot_layout(owners, slot_count, total_slot_count):
    block_count = owners.shape[0]
    slot_position = jnp.arange(block_count, dtype=jnp.int32)
    before = (owners[:, None] == owners[None, :]) & (
        slot_position[:, None] > slot_position[None, :]
    )
    rank_in = jnp.sum(before.astype(jnp.int32), axis=1)
    target = owners * slot_count + rank_in
    matches = (target[:, None] == jnp.arange(total_slot_count, dtype=jnp.int32)[None, :]).astype(
        jnp.int32
    )
    source = jnp.sum(matches * slot_position[:, None], axis=0)
    occupied = jnp.sum(matches, axis=0)
    return (target, source, occupied)


def soap_update(
    gradient, occupied, moment, second, stat_left, stat_right, basis_left, basis_right, step_count
):
    elapsed = step_count[0].astype(jnp.float32)
    moment_new = 0.95 * moment + 0.05 * gradient
    rotated = product(transposed(basis_left), product(gradient, basis_right))
    rot_moment = product(transposed(basis_left), product(moment_new, basis_right))
    second_new = 0.95 * second + 0.05 * rotated * rotated
    correction = 1.0 - jnp.power(jnp.float32(0.95), elapsed)
    scaled = rot_moment / correction / (jnp.sqrt(second_new / correction) + 1e-08)
    occupied_mask = (occupied > 0)[:, None, None]
    direction = jnp.where(
        occupied_mask, product(basis_left, product(scaled, transposed(basis_right))), 0.0
    )
    left_stat = 0.95 * stat_left + 0.05 * product(gradient, transposed(gradient))
    right_stat = 0.95 * stat_right + 0.05 * product(transposed(gradient), gradient)
    left_new = jnp.where(occupied_mask, refresh(left_stat, basis_left), basis_left)
    right_new = jnp.where(occupied_mask, refresh(right_stat, basis_right), basis_right)
    return (direction, left_new, right_new)


def body(
    partials,
    owners,
    step_count,
    master,
    moment,
    second,
    stat_left,
    stat_right,
    basis_left,
    basis_right,
):
    owner_count = lax.axis_size("owner")
    slot_count = master.shape[0]
    total_slot_count = slot_count * owner_count
    target, source, occupied = slot_layout(owners, slot_count, total_slot_count)
    first_slot = lax.axis_index("owner") * slot_count
    occupied_mine = lax.dynamic_slice_in_dim(occupied, first_slot, slot_count, 0)
    own_part = partials[0]
    mask_all = (occupied > 0).astype(jnp.float32)[:, None, None]
    placed = jnp.take(own_part, source, axis=0).astype(jnp.float32) * mask_all
    summed = lax.psum_scatter(placed.astype(jnp.bfloat16), "owner", scatter_dimension=0, tiled=True)
    gradient = lax.psum(summed, "dp").astype(jnp.float32)
    direction, left_new, right_new = soap_update(
        gradient,
        occupied_mine,
        moment,
        second,
        stat_left,
        stat_right,
        basis_left,
        basis_right,
        step_count,
    )
    updated = (master - 0.01 * (direction + 0.1 * master)).astype(jnp.bfloat16)
    every_slot = lax.all_gather(updated, "owner", axis=0, tiled=True)
    weights_all = jnp.take(every_slot, target, axis=0)
    return (weights_all, direction, left_new, right_new)


def solution(mesh):
    placed = (
        P(("dp", "owner"), None, None, None),
        P(),
        P(),
        P("owner", None, None),
        P("owner", None, None),
        P("owner", None, None),
        P("owner", None, None),
        P("owner", None, None),
        P("owner", None, None),
        P("owner", None, None),
    )
    return jax.shard_map(
        body,
        mesh=mesh,
        in_specs=placed,
        out_specs=(P(), P("owner", None, None), P("owner", None, None), P("owner", None, None)),
        check_vma=False,
    )
```

profile of v0, /device:TPU:1, one launch (start us, length us, event | category | flops | bytes accessed | tf_op | source)
XLA Modules:
  0.0 320.2 jit_solution(9611837866176556709)
XLA Ops:
  7.2 1.0 convert_reduce_fusion.1
  9.1 8.0 %gather_fusion = bf16[192,128,128]{2,1,0:T(8,128)(2,1)} fusion(bf16[96,128,128]{2,1,0:T(8,128)(2,1)S(1)} %bitcast.85, s32[1024]{0:T(1024)S(1)} %pad_clamp_fusion.1), kind=kCustom, calls=%fused_computation | custom fusion | bytes 12583680 | tf_op jit(solution)/shard_map/jit(_take)/gather | solution.py:83
  17.1 8.6 %copy.70 = bf16[192,128,128]{1,2,0:T(8,128)(2,1)} copy(bf16[192,128,128]{2,1,0:T(8,128)(2,1)} %gather_fusion) | data formatting | bytes 12582912 | tf_op jit(solution)/shard_map/jit(_take)/gather | solution.py:83
  25.7 7.5 %multiply_convert_fusion = bf16[192,128,128]{1,2,0:T(8,128)(2,1)} fusion(f32[192]{0:T(256)S(1)} %get-tuple-element.30, bf16[192,128,128]{1,2,0:T(8,128)(2,1)} %copy.70, pred[192]{0:T(512)(128)(4,1)S(1)} %get-tuple-element.31), kind=kLoop, calls=%fused_computation.2 | loop fusion | flops 12582912 | bytes 12583872 | tf_op jit(solution)/shard_map/convert_element_type | solution.py:84
  33.3 112.5 %reduce-scatter.2.cloned.1.call-done = bf16[6,128,128]{1,2,0:T(8,128)(2,1)} async-done(((bf16[192,128,128]{1,2,0:T(8,128)(2,1)}), bf16[6,128,128]{1,2,0:T(8,128)(2,1)}) %reduce-scatter.2.cloned.1.call-update) | async-done | bytes 196624 | tf_op jit(solution)/shard_map/reduce_scatter | solution.py:84
  146.0 1.9 copy.73
  148.5 1.9 copy.69
  150.5 1.9 copy.79
  152.5 67.6 %all-reduce.2.cloned.1.call-done = bf16[6,128,128]{1,2,0:T(8,128)(2,1)} async-done(((bf16[6,128,128]{1,2,0:T(8,128)(2,1)}), bf16[6,128,128]{1,2,0:T(8,128)(2,1)}) %all-reduce.2.cloned.1.call-update) | async-done | bytes 196624 | tf_op jit(solution)/shard_map/psum | solution.py:85
  220.1 1.5 fusion.35
  221.6 1.8 fusion.22
  223.4 1.9 fusion.23
  225.3 1.5 fusion
  227.3 1.8 subtract_convert_fusion
  229.1 1.7 copy.80
  230.9 1.9 copy.92
  232.8 1.9 copy.81
  234.7 1.9 copy.102
  236.6 1.5 fusion.2
  238.1 0.9 multiply_reduce_fusion
  239.0 1.5 fusion.1
  240.5 1.9 multiply_reduce_fusion.1
  242.4 0.9 fusion.31
  243.3 0.9 fusion.30
  247.6 1.0 fusion.44
  252.0 0.8 fusion.37
  256.1 0.8 fusion.40
  258.3 1.3 fusion.4
  259.7 1.3 fusion.11
  261.0 43.3 %all-gather.2.cloned.1.call-done = bf16[192,128,128]{2,1,0:T(8,128)(2,1)} async-done(((bf16[6,128,128]{2,1,0:T(8,128)(2,1)}), bf16[192,128,128]{2,1,0:T(8,128)(2,1)}) %all-gather.2.cloned.1.call-update) | async-done | bytes 6291472 | tf_op jit(solution)/shard_map/all_gather | solution.py:98
  304.3 5.5 %gather_fusion.1 = bf16[96,128,128]{2,1,0:T(8,128)(2,1)} fusion(bf16[192,128,128]{2,1,0:T(8,128)(2,1)} %all-gather.2.cloned.1.call-done, s32[1024]{0:T(1024)S(1)} %pad_clamp_fusion), kind=kCustom, calls=%fused_computation.1 | custom fusion | bytes 6291840 | tf_op jit(solution)/shard_map/jit(_take)/gather | solution.py:99
  309.8 3.9 %broadcast_select_fusion = bf16[96,128,128]{2,1,0:T(8,128)(2,1)} fusion(bf16[96,128,128]{2,1,0:T(8,128)(2,1)} %gather_fusion.1, pred[96]{0:T(512)(128)(4,1)S(1)} %get-tuple-element.22), kind=kLoop, calls=%fused_computation.3 | loop fusion | flops 1572864 | bytes 6291552 | tf_op jit(solution)/shard_map/jit(_take)/select_n | solution.py:99
  (44 shorter events, 13.2 us)
Async XLA Ops:
  7.2 1.9 copy-start
  7.2 138.6 %reduce-scatter.2.cloned.1.call-start = ((), (), s32[]{:S(2)}) async-start(), calls=%async_computation.1 | async-start | bytes 6488064 | tf_op jit(solution)/shard_map/reduce_scatter | solution.py:84
  33.2 186.9 %copy-start.1 = (f32[6,128,128]{2,1,0:T(8,128)S(1)}, f32[6,128,128]{2,1,0:T(8,128)}, u32[]{:S(2)}) copy-start(f32[6,128,128]{2,1,0:T(8,128)} %param.19) | copy-start | bytes 1179652
  33.2 186.8 %all-reduce.2.cloned.1.call-start = ((), (), s32[]{:S(2)}) async-start(), calls=%async_computation.2 | async-start | bytes 393216 | tf_op jit(solution)/shard_map/psum | solution.py:85
  145.8 158.6 %all-gather.2.cloned.1.call-start = ((), (), s32[]{:S(2)}) async-start(), calls=%async_computation.3 | async-start | bytes 6488064 | tf_op jit(solution)/shard_map/all_gather | solution.py:98
  220.1 7.2 %copy-start.2 = (f32[6,128,128]{2,1,0:T(8,128)S(1)}, f32[6,128,128]{2,1,0:T(8,128)}, u32[]{:S(2)}) copy-start(f32[6,128,128]{2,1,0:T(8,128)} %param.18) | copy-start | bytes 1179652
  220.1 7.2 %copy-start.4 = (f32[6,128,128]{1,2,0:T(8,128)S(1)}, f32[6,128,128]{1,2,0:T(8,128)}, u32[]{:S(2)}) copy-start(f32[6,128,128]{1,2,0:T(8,128)} %copy.79) | copy-start | bytes 1179652
  252.0 7.7 %copy-start.3 = (f32[6,128,128]{2,1,0:T(8,128)S(1)}, f32[6,128,128]{2,1,0:T(8,128)}, u32[]{:S(2)}) copy-start(f32[6,128,128]{2,1,0:T(8,128)} %param.18) | copy-start | bytes 1179652
Sparse Core Ops, SparseCore 0:
  33.3 112.3 reduce-scatter.1
  148.5 71.5 all-reduce.1
  231.0 73.2 all-gather.1
where the time goes:
time: 321 us; the launch traced here: 320 us
  waiting for transfers between devices  223 us (69%)
  local copies, waits for them, and re-layouts  35.4 us (11%)
  matrix products  33.2 us (10%)
  between operations  14.7 us (5%)
  other arithmetic  13.3 us (4%)
    reduce_scatter x1, waiting for transfers between devices, body(): lax.psum_scatter(placed.astype(jnp.bfloat16), 'owner', scatter_dimension=...  112 us
    psum x1, waiting for transfers between devices, body(): gradient = lax.psum(summed, 'dp').astype(jnp.float32)  67.6 us
    all_gather x1, waiting for transfers between devices, body(): every_slot = lax.all_gather(updated, 'owner', axis=0, tiled=True)  43.3 us
    dot_general x34, matrix products, product(): return jnp.matmul(left, right, precision=lax.Precision.HIGHEST)  33.2 us
    gather x2, local copies, waits for them, and re-layouts, body(): placed = jnp.take(own_part, source, axis=0).astype(jnp.float32) * mask_all  16.6 us
    unnamed x16, local copies, waits for them, and re-layouts  11.5 us
    convert_element_type x1, other arithmetic, body(): placed.astype(jnp.bfloat16)  7.46 us
  transfers between devices with their start and end apart: 3, of which 3 were waited for; matrix products, arithmetic and copies ran while one was open for 11% of the time, Pallas kernels for 0%

commit v1 on v0

--- a/solution.py
+++ b/solution.py
@@ -4,6 +4,11 @@
 from jax.sharding import PartitionSpec as P
 
 NS_ITERS = 6
+
+
+def summed_here(x, axis):
+    parts = lax.all_gather(x, axis)
+    return jnp.sum(parts, axis=0)
 
 
 def product(left, right):
@@ -82,7 +87,7 @@
     mask_all = (occupied > 0).astype(jnp.float32)[:, None, None]
     placed = jnp.take(own_part, source, axis=0).astype(jnp.float32) * mask_all
     summed = lax.psum_scatter(placed.astype(jnp.bfloat16), "owner", scatter_dimension=0, tiled=True)
-    gradient = lax.psum(summed, "dp").astype(jnp.float32)
+    gradient = summed_here(summed, "dp").astype(jnp.float32)
     direction, left_new, right_new = soap_update(
         gradient,
         occupied_mine,

time: 321 us -> 284 us (0.88)
  waiting for transfers between devices: 223 us -> 190 us
  local copies, waits for them, and re-layouts: 35.4 us -> 28.5 us
    psum x1 -> x0, waiting for transfers between devices: 67.6 us -> none  [body(): gradient = lax.psum(summed, 'dp').astype(jnp.float32)]
    all_gather x0 -> x1, waiting for transfers between devices: none -> 37.6 us  [summed_here(): parts = lax.all_gather(x, axis)]
    gather x2 -> x1, local copies, waits for them, and re-layouts: 16.6 us -> 8.01 us  [body(): placed = jnp.take(own_part, source, axis=0).astype(jnp.float32) * mask_all]
  transfers between devices with their start and end apart: 3 -> 3, of which waited for: 3 -> 3; matrix products, arithmetic and copies ran while one was open for 11% -> 13% of each run, Pallas kernels for 0% -> 0%
where the time goes in v1:
time: 284 us; the launch traced here: 283 us
  waiting for transfers between devices  190 us (67%)
  matrix products  33 us (12%)
  local copies, waits for them, and re-layouts  28.5 us (10%)
  other arithmetic  15.7 us (6%)
  between operations  14.9 us (5%)
    reduce_scatter x1, waiting for transfers between devices, body(): lax.psum_scatter(placed.astype(jnp.bfloat16), 'owner', scatter_dimension=...  112 us
    all_gather x1, waiting for transfers between devices, body(): every_slot = lax.all_gather(updated, 'owner', axis=0, tiled=True)  40.4 us
    all_gather x1, waiting for transfers between devices, summed_here(): parts = lax.all_gather(x, axis)  37.6 us
    dot_general x34, matrix products, product(): return jnp.matmul(left, right, precision=lax.Precision.HIGHEST)  33 us
    unnamed x16, local copies, waits for them, and re-layouts  11.5 us
    gather x1, local copies, waits for them, and re-layouts, body(): placed = jnp.take(own_part, source, axis=0).astype(jnp.float32) * mask_all  8.01 us
    convert_element_type x1, other arithmetic, body(): placed.astype(jnp.bfloat16)  7.5 us
  transfers between devices with their start and end apart: 3, of which 3 were waited for; matrix products, arithmetic and copies ran while one was open for 13% of the time, Pallas kernels for 0%

profile of v1, /device:TPU:1, one launch (start us, length us, event | category | flops | bytes accessed | tf_op | source)
XLA Modules:
  0.0 282.8 jit_solution(10120646255417960455)
XLA Ops:
  7.2 1.0 convert_reduce_fusion.1
  9.1 8.0 %gather_fusion = bf16[192,128,128]{2,1,0:T(8,128)(2,1)} fusion(bf16[96,128,128]{2,1,0:T(8,128)(2,1)S(1)} %bitcast.86, s32[1024]{0:T(1024)S(1)} %pad_clamp_fusion.1), kind=kCustom, calls=%fused_computation | custom fusion | bytes 12583680 | tf_op jit(solution)/shard_map/jit(_take)/gather | solution.py:88
  17.1 7.5 %multiply_convert_fusion = bf16[192,128,128]{2,1,0:T(8,128)(2,1)} fusion(f32[192]{0:T(256)S(1)} %get-tuple-element.30, bf16[192,128,128]{2,1,0:T(8,128)(2,1)} %gather_fusion, pred[192]{0:T(512)(128)(4,1)S(1)} %get-tuple-element.31), kind=kLoop, calls=%fused_computation.2 | loop fusion | flops 12582912 | bytes 12583872 | tf_op jit(solution)/shard_map/convert_element_type | solution.py:89
  24.7 112.4 %reduce-scatter.2.cloned.1.call-done = bf16[6,128,128]{2,1,0:T(8,128)(2,1)} async-done(((bf16[192,128,128]{2,1,0:T(8,128)(2,1)}), bf16[6,128,128]{2,1,0:T(8,128)(2,1)}) %reduce-scatter.2.cloned.1.call-update) | async-done | bytes 196624 | tf_op jit(solution)/shard_map/reduce_scatter | solution.py:89
  137.3 1.9 copy.74
  139.2 1.9 copy.69
  141.8 1.9 copy.65
  143.8 37.6 %all-gather.6.cloned.1.call-done = bf16[48,128,128]{2,1,0:T(8,128)(2,1)} async-done(((bf16[6,128,128]{2,1,0:T(8,128)(2,1)}), bf16[48,128,128]{2,1,0:T(8,128)(2,1)}) %all-gather.6.cloned.1.call-update) | async-done | bytes 1572880 | tf_op jit(solution)/shard_map/all_gather | solution.py:10
  181.4 2.4 reduce_sum.63
  183.8 1.7 copy.66
  185.5 1.5 fusion.35
  187.0 1.9 fusion.23
  188.9 1.8 fusion.22
  190.7 1.5 fusion
  192.8 1.8 subtract_convert_fusion
  194.6 1.7 copy.75
  196.3 1.9 copy.76
  198.2 1.9 copy.85
  200.2 1.9 copy.95
  202.1 1.5 fusion.1
  203.5 1.9 multiply_reduce_fusion.1
  205.4 1.5 fusion.2
  206.9 0.9 multiply_reduce_fusion
  207.8 0.9 fusion.30
  208.7 0.9 fusion.31
  213.2 0.8 fusion.39
  214.6 0.8 fusion.40
  223.8 1.3 fusion.11
  225.2 1.3 fusion.4
  226.5 40.4 %all-gather.4.cloned.1.call-done = bf16[192,128,128]{2,1,0:T(8,128)(2,1)} async-done(((bf16[6,128,128]{2,1,0:T(8,128)(2,1)}), bf16[192,128,128]{2,1,0:T(8,128)(2,1)}) %all-gather.4.cloned.1.call-update) | async-done | bytes 6291472 | tf_op jit(solution)/shard_map/all_gather | solution.py:103
  266.9 5.5 %gather_fusion.1 = bf16[96,128,128]{2,1,0:T(8,128)(2,1)} fusion(bf16[192,128,128]{2,1,0:T(8,128)(2,1)} %all-gather.4.cloned.1.call-done, s32[1024]{0:T(1024)S(1)} %pad_clamp_fusion), kind=kCustom, calls=%fused_computation.1 | custom fusion | bytes 6291840 | tf_op jit(solution)/shard_map/jit(_take)/gather | solution.py:104
  272.4 3.9 %broadcast_select_fusion = bf16[96,128,128]{2,1,0:T(8,128)(2,1)} fusion(bf16[96,128,128]{2,1,0:T(8,128)(2,1)} %gather_fusion.1, pred[96]{0:T(512)(128)(4,1)S(1)} %get-tuple-element.22), kind=kLoop, calls=%fused_computation.3 | loop fusion | flops 1572864 | bytes 6291552 | tf_op jit(solution)/shard_map/jit(_take)/select_n | solution.py:104
  (45 shorter events, 14.0 us)
Async XLA Ops:
  7.2 1.9 copy-start
  7.2 129.9 %reduce-scatter.2.cloned.1.call-start = ((), (), s32[]{:S(2)}) async-start(), calls=%async_computation.1 | async-start | bytes 6488064 | tf_op jit(solution)/shard_map/reduce_scatter | solution.py:89
  24.6 160.9 %copy-start.1 = (f32[6,128,128]{2,1,0:T(8,128)S(1)}, f32[6,128,128]{2,1,0:T(8,128)}, u32[]{:S(2)}) copy-start(f32[6,128,128]{2,1,0:T(8,128)} %param.19) | copy-start | bytes 1179652
  24.6 156.8 %all-gather.6.cloned.1.call-start = ((), (), s32[]{:S(2)}) async-start(), calls=%async_computation.3 | async-start | bytes 1769472 | tf_op jit(solution)/shard_map/all_gather | solution.py:10
  137.1 129.8 %all-gather.4.cloned.1.call-start = ((), (), s32[]{:S(2)}) async-start(), calls=%async_computation.2 | async-start | bytes 6488064 | tf_op jit(solution)/shard_map/all_gather | solution.py:103
  185.5 7.2 %copy-start.2 = (f32[6,128,128]{2,1,0:T(8,128)S(1)}, f32[6,128,128]{2,1,0:T(8,128)}, u32[]{:S(2)}) copy-start(f32[6,128,128]{2,1,0:T(8,128)} %param.18) | copy-start | bytes 1179652
  185.5 7.2 %copy-start.4 = (f32[6,128,128]{1,2,0:T(8,128)S(1)}, f32[6,128,128]{1,2,0:T(8,128)}, u32[]{:S(2)}) copy-start(f32[6,128,128]{1,2,0:T(8,128)} %copy.74) | copy-start | bytes 1179652
  216.8 7.0 %copy-start.3 = (f32[6,128,128]{2,1,0:T(8,128)S(1)}, f32[6,128,128]{2,1,0:T(8,128)}, u32[]{:S(2)}) copy-start(f32[6,128,128]{2,1,0:T(8,128)} %param.18) | copy-start | bytes 1179652
Sparse Core Ops, SparseCore 0:
  24.8 112.2 reduce-scatter.1
  139.0 42.3 all-gather.5
  196.4 70.3 all-gather.3
